TPU v7x, 32 devices: a whole 2x2x4 slice. The times are simulated.
32 devices in a mesh: dp: 8 (over z, x), tensor: 4 (over y, core).
Axes of the slice: x: 2, y: 2, z: 4, core: 2. Of those that a mesh axis runs over, the one named last changes fastest.
Arguments:
- inputs: bfloat16 [16, 1024, 1024], P('dp'), may hold values from -6 to 6
- segment_ids: int32 [16, 1024], P('dp'), may hold values from 0 to 7, never falling along the last dimension, each value on 1 to 512 neighbouring positions
- doc_offsets: int32 [16, 8], P('dp'), may hold values from 0 to 3071
- time_index: int32 [16], P('dp'), may hold values from 0 to 999
- w_qkv: bfloat16 [3, 1024, 1024], P(None, 'dp', 'tensor'), may hold values from -0.1875 to 0.1875
- w_out: bfloat16 [1024, 1024], P('tensor', 'dp'), may hold values from -0.75 to 0.75
- w_up: bfloat16 [1024, 4096], P('dp', 'tensor'), may hold values from -0.1875 to 0.1875
- w_down: bfloat16 [4096, 1024], P('tensor', 'dp'), may hold values from -0.09375 to 0.09375
- w_time: bfloat16 [256, 1024], P(None, 'dp'), may hold values from -0.375 to 0.375
- gain_attn: bfloat16 [1024], P('dp'), may hold values from 0.5 to 1.5
- gain_mlp: bfloat16 [1024], P('dp'), may hold values from 0.5 to 1.5
- cotangent: bfloat16 [16, 1024, 1024], P('dp'), may hold values from -6 to 6
Outputs:
- block_out: bfloat16 [16, 1024, 1024], P('dp', None, 'tensor')
- input_grad: float32 [16, 1024, 1024], P('dp', None, 'tensor')
- grad_qkv: float32 [3, 1024, 1024], P(None, 'dp', 'tensor')
- grad_out: float32 [1024, 1024], P('tensor', 'dp')
- grad_up: float32 [1024, 4096], P('dp', 'tensor')
- grad_down: float32 [4096, 1024], P('tensor', 'dp')
- grad_time: float32 [256, 1024], P(None, 'dp')
- grad_gain_attn: float32 [1024], P('dp')
- grad_gain_mlp: float32 [1024], P('dp')
Inputs may be any that keep to these rules, and one draw needn't show every extreme that they name: `segment_ids`: in each sequence the ids never fall, every id of 0 to 7 occurs, each document has 1 to 512 tokens and one has exactly 512.
All inputs are finite; a program needn't handle non-finite values.
Results may differ from a plain program's by a relative error of at most 0.022.
Values may be sent and summed in bfloat16 or wider, within the bound.
No kernel may reach another device: no remote copies, remote signals or barrier semaphores. Data moves between devices by JAX's collectives and lax.ppermute only.
A program may use at most 192 MiB of HBM per device.

v0:
```python
import math
import jax
import jax.numpy as jnp
from jax import lax
from jax.sharding import PartitionSpec as P

HEADS = 16
TEMB = 256
eps = 1e-05
masked = -1000000000.0
f32 = jnp.float32
bf16 = jnp.bfloat16


def sinusoid(values, width):
    half = width // 2
    freqs = jnp.exp(-math.log(10000.0) * jnp.arange(half, dtype=f32) / half)
    angles = values[..., None] * freqs
    return jnp.concatenate([jnp.sin(angles), jnp.cos(angles)], axis=-1)


def norm_parts(hidden):
    centre = jnp.mean(hidden, axis=-1, keepdims=True)
    centred = hidden - centre
    spread = jnp.mean(centred * centred, axis=-1, keepdims=True)
    inv = lax.rsqrt(spread + eps)
    return (centred * inv, inv)


def norm_back(unit, inv, gain, grad):
    scaled = grad * gain
    first = jnp.mean(scaled, axis=-1, keepdims=True)
    second = jnp.mean(scaled * unit, axis=-1, keepdims=True)
    return inv * (scaled - first - unit * second)


def positions(segs, offsets):
    seq_len = segs.shape[0]
    index = jnp.arange(seq_len, dtype=jnp.int32)
    member = segs[:, None] == jnp.arange(offsets.shape[0], dtype=jnp.int32)[None, :]
    starts = jnp.min(jnp.where(member, index[:, None], seq_len), axis=0)
    start_tok = jnp.sum(jnp.where(member, starts[None, :], 0), axis=1)
    offset_tok = jnp.sum(jnp.where(member, offsets[None, :], 0), axis=1)
    return offset_tok + index - start_tok


def attend(query, key, value, same, scale):
    scores = jnp.einsum("qhe,khe->hqk", query, key, preferred_element_type=f32) * scale
    scores = jnp.where(same[None], scores, masked)
    top = jnp.max(scores, axis=-1, keepdims=True)
    expo = jnp.exp(scores - top)
    denom = jnp.sum(expo, axis=-1, keepdims=True)
    probs = (expo / denom).astype(bf16)
    out = jnp.einsum("hqk,khe->qhe", probs, value, preferred_element_type=f32)
    return (out, top + jnp.log(denom))


def attend_back(query, key, value, same, scale, lse, d_mixed):
    scores = jnp.einsum("qhe,khe->hqk", query, key, preferred_element_type=f32) * scale
    scores = jnp.where(same[None], scores, masked)
    probs = jnp.exp(scores - lse)
    d_probs = jnp.einsum("qhe,khe->hqk", d_mixed, value, preferred_element_type=f32)
    d_value = jnp.einsum("hqk,qhe->khe", probs.astype(bf16), d_mixed, preferred_element_type=f32)
    delta = jnp.sum(probs * d_probs, axis=-1, keepdims=True)
    d_scores = (probs * (d_probs - delta)).astype(bf16)
    d_query = jnp.einsum("hqk,khe->qhe", d_scores, key, preferred_element_type=f32) * scale
    d_key = jnp.einsum("hqk,qhe->khe", d_scores, query, preferred_element_type=f32) * scale
    return (d_query, d_key, d_value)


def mm(left, right):
    return jnp.dot(left, right, preferred_element_type=f32)


def mm_rt(left, right):
    return jnp.einsum("ik,jk->ij", left, right, preferred_element_type=f32)


def mm_lt(left, right):
    return jnp.einsum("ki,kj->ij", left, right, preferred_element_type=f32)


class Ring:

    def __init__(self, n):
        self.n = n
        self.order = list(range(0, n, 2)) + list(range(n - 1, 0, -2))
        inverse = [self.order.index(i) for i in range(n)]
        self.me = lax.axis_index("dp")
        self.spot = jnp.array(inverse, jnp.int32)[self.me]
        self.table = jnp.array(self.order, jnp.int32)
        self.right = [(self.order[p], self.order[(p + 1) % n]) for p in range(n)]
        self.left = [(b, a) for a, b in self.right]

    def at(self, offset):
        return self.table[(self.spot + offset) % self.n]

    def gather(self, block):
        rows = block.shape[0]
        full = jnp.zeros((self.n * rows,) + block.shape[1:], block.dtype)
        full = lax.dynamic_update_slice_in_dim(full, block, self.me * rows, 0)
        from_left = from_right = block
        for hop in range(1, self.n // 2 + 1):
            from_left = lax.ppermute(from_left, "dp", self.right)
            if hop <= self.n - 1 - self.n // 2:
                from_right = lax.ppermute(from_right, "dp", self.left)
                full = lax.dynamic_update_slice_in_dim(full, from_right, self.at(hop) * rows, 0)
            full = lax.dynamic_update_slice_in_dim(full, from_left, self.at(-hop) * rows, 0)
        return full

    def scatter(self, full):
        rows = full.shape[0] // self.n

        def part(offset):
            return lax.dynamic_slice_in_dim(full, self.at(offset) * rows, rows, 0).astype(f32)

        total = part(0)
        for hops, way, sign in (
            (self.n // 2, self.right, 1),
            (self.n - 1 - self.n // 2, self.left, -1),
        ):
            run = part(sign * hops)
            for hop in range(1, hops + 1):
                run = lax.ppermute(run.astype(bf16), "dp", way).astype(f32)
                if hop < hops:
                    run = run + part(sign * (hops - hop))
            if hops:
                total = total + run
        return total


def swap(value, bit, n):
    return lax.ppermute(value, "tensor", [(i, i ^ bit) for i in range(n)])


def to_features(value, n):
    me = lax.axis_index("tensor")
    tokens, width = value.shape
    value = value.reshape(tokens, n, width // n)
    bit = 1
    while bit < n:
        value = value.reshape(tokens, -1, 2, width // n)
        mine = me // bit % 2
        keep = lax.dynamic_index_in_dim(value, mine, 2, keepdims=False)
        send = lax.dynamic_index_in_dim(value, 1 - mine, 2, keepdims=False)
        got = swap(send.astype(bf16), bit, n).astype(f32)
        if bit == 1:
            got = jnp.concatenate([got[tokens // 2 :], got[: tokens // 2]], axis=0)
        value = keep.astype(f32) + got
        bit *= 2
    return value.reshape(tokens, width // n)


def shards(
    inputs,
    segment_ids,
    doc_offsets,
    time_index,
    w_qkv,
    w_out,
    w_up,
    w_down,
    w_time,
    gain_attn,
    gain_mlp,
    cotangent,
):
    n_dp = lax.axis_size("dp")
    n_tensor = lax.axis_size("tensor")
    me_dp = lax.axis_index("dp")
    core = lax.axis_index("tensor") % 2
    chips = n_tensor // 2
    seqs_dev, seq_len, width = inputs.shape
    half = seq_len // 2
    shard = width // n_tensor
    head_size = width // HEADS
    heads_dev = shard // head_size
    scale = head_size ** (-0.5)
    hidden_dev = w_up.shape[1]
    ring = Ring(n_dp)
    w1_part = jnp.concatenate([w_qkv[0], w_qkv[1], w_qkv[2], w_out.T], axis=1)
    w1 = ring.gather(w1_part)
    w2_part = jnp.concatenate([w_up, w_down.T], axis=1)
    w2 = lax.all_gather(w2_part, "dp", axis=0, tiled=True)
    times = lax.all_gather(time_index, "dp", axis=0, tiled=True)
    temb = sinusoid(times.astype(f32), TEMB)
    cond_part = jnp.dot(temb, w_time.astype(f32), precision=lax.Precision.HIGHEST)
    small = jnp.concatenate(
        [cond_part, gain_attn.astype(f32)[None], gain_mlp.astype(f32)[None]], axis=0
    )
    small = lax.all_gather(small, "dp", axis=1, tiled=True)
    n_seqs = n_dp * seqs_dev
    cond = lax.dynamic_slice_in_dim(small, me_dp * seqs_dev, seqs_dev, 0)
    attn_g, mlp_g = (small[n_seqs], small[n_seqs + 1])

    def own_first(value):
        return jnp.roll(value, -core * half, axis=0)

    def exchange_core(value):
        return swap(value, 1, n_tensor)

    def sum_chips(value):
        bit = 2
        value = value.astype(f32)
        while bit < n_tensor:
            low = value.astype(bf16)
            value = low.astype(f32) + swap(low, bit, n_tensor).astype(f32)
            bit *= 2
        return value

    seqs = range(seqs_dev)
    cot = [own_first(cotangent[i]) for i in seqs]
    segs = [own_first(segment_ids[i]) for i in seqs]
    same = [s[:, None] == s[None, :] for s in segs]
    h0, unit0, inv0, n1 = ([], [], [], [])
    for i in seqs:
        place = own_first(positions(segment_ids[i], doc_offsets[i]))
        h = own_first(inputs[i]).astype(f32) + sinusoid(place.astype(f32), width) + cond[i][None]
        unit, inv = norm_parts(h)
        h0.append(h)
        unit0.append(unit)
        inv0.append(inv)
        n1.append((unit * attn_g).astype(bf16))
    query, key, value, mixed, lse = ([], [], [], [], [])
    h1, unit1, inv1, n2 = ([], [], [], [])
    for i in seqs:
        qkv = mm(n1[i], w1[:, : 3 * shard]).astype(bf16)
        heads = [
            qkv[:, c * shard : (c + 1) * shard].reshape(seq_len, heads_dev, head_size)
            for c in range(3)
        ]
        out, total = attend(*heads, same[i], scale)
        out = out.reshape(seq_len, shard).astype(bf16)
        send = mm_rt(out[half:], w1[:, 3 * shard :]).astype(bf16)
        keep = mm_rt(out[:half], w1[:, 3 * shard :]).astype(bf16)
        attn = sum_chips(keep.astype(f32) + exchange_core(send).astype(f32))
        h = h0[i][:half] + attn
        unit, inv = norm_parts(h)
        own = (unit * mlp_g).astype(bf16)
        query.append(heads[0])
        key.append(heads[1])
        value.append(heads[2])
        mixed.append(out)
        lse.append(total)
        h1.append(h)
        unit1.append(unit)
        inv1.append(inv)
        n2.append(jnp.concatenate([own, exchange_core(own)], axis=0))
    w_up_full, w_down_t = (w2[:, :hidden_dev], w2[:, hidden_dev:])
    active, d_hidden, d_h1, d_h1_low, block_out = ([], [], [], [], [])
    gain_mlp_sum = jnp.zeros((width,), f32)
    for i in seqs:
        hidden = mm(n2[i], w_up_full)
        d_active = mm(cot[i], w_down_t)
        erf = lax.erf(hidden * 0.5**0.5)
        cdf = 0.5 + 0.5 * erf
        active.append((hidden * cdf).astype(bf16))
        slope = cdf + hidden * jnp.exp(-0.5 * hidden * hidden) * (0.5 / math.pi) ** 0.5
        d_hidden.append((d_active * slope).astype(bf16))
        d_n2_send = mm_rt(d_hidden[i][half:], w_up_full).astype(bf16)
        d_n2_keep = mm_rt(d_hidden[i][:half], w_up_full).astype(bf16)
        d_n2 = sum_chips(d_n2_keep.astype(f32) + exchange_core(d_n2_send).astype(f32))
        gain_mlp_sum = gain_mlp_sum + jnp.sum(d_n2 * unit1[i], axis=0)
        d_h1.append(cot[i][:half].astype(f32) + norm_back(unit1[i], inv1[i], mlp_g, d_n2))
        low = d_h1[i].astype(bf16)
        d_h1_low.append(jnp.concatenate([low, exchange_core(low)], axis=0))
        term = mm_rt(active[i], w_down_t)
        term = jnp.concatenate([term[:half] + h1[i] * (1.0 / chips), term[half:]], axis=0)
        block_out.append(to_features(term.astype(bf16), n_tensor).astype(bf16))
    cot_all = jnp.concatenate(cot, axis=0)
    grad2 = jnp.concatenate(
        [
            mm_lt(jnp.concatenate(n2, axis=0), jnp.concatenate(d_hidden, axis=0)).astype(bf16),
            mm_lt(cot_all, jnp.concatenate(active, axis=0)).astype(bf16),
        ],
        axis=1,
    )
    share2 = lax.psum_scatter(grad2, "dp", scatter_dimension=0, tiled=True).astype(f32)
    d_qkv, input_grad, seq_sums = ([], [], [])
    gain_attn_sum = jnp.zeros((width,), f32)
    for i in seqs:
        d_mixed = mm(d_h1_low[i], w1[:, 3 * shard :]).astype(bf16)
        parts = attend_back(
            query[i],
            key[i],
            value[i],
            same[i],
            scale,
            lse[i],
            d_mixed.reshape(seq_len, heads_dev, head_size),
        )
        d_qkv.append(
            jnp.concatenate([p.reshape(seq_len, shard).astype(bf16) for p in parts], axis=1)
        )
        d_n1 = mm_rt(d_qkv[i], w1[:, : 3 * shard])
        gain_attn_sum = gain_attn_sum + jnp.sum(d_n1 * unit0[i], axis=0)
        term = norm_back(unit0[i], inv0[i], attn_g, d_n1)
        term = jnp.concatenate([term[:half] + d_h1[i] * (1.0 / chips), term[half:]], axis=0)
        seq_sums.append(jnp.sum(term, axis=0))
        input_grad.append(to_features(term.astype(bf16), n_tensor))
    grad1 = jnp.concatenate(
        [
            mm_lt(jnp.concatenate(n1, axis=0), jnp.concatenate(d_qkv, axis=0)).astype(bf16),
            mm_lt(jnp.concatenate(d_h1_low, axis=0), jnp.concatenate(mixed, axis=0)).astype(bf16),
        ],
        axis=1,
    )
    share1 = ring.scatter(grad1)
    sums = jnp.zeros((n_seqs, width), f32)
    sums = lax.dynamic_update_slice_in_dim(sums, jnp.stack(seq_sums), me_dp * seqs_dev, 0)
    sums = jnp.concatenate([sums, gain_attn_sum[None], gain_mlp_sum[None] * (1.0 / chips)], axis=0)
    sums = lax.psum(sums, ("dp", "tensor"))
    rows = width // n_dp
    sums = lax.dynamic_slice_in_dim(sums, me_dp * rows, rows, 1)
    factor = float(n_seqs * seq_len) ** (-0.5)
    grad_time = (
        jnp.einsum("st,sd->td", temb, sums[:n_seqs], precision=lax.Precision.HIGHEST) * factor
    )

    def natural(value):
        return jnp.roll(value, core * half, axis=0)

    share1, share2 = (share1 * factor, share2 * factor)
    return (
        jnp.stack([natural(b) for b in block_out]),
        jnp.stack([natural(g) for g in input_grad]),
        jnp.stack([share1[:, c * shard : (c + 1) * shard] for c in range(3)]),
        share1[:, 3 * shard :].T,
        share2[:, :hidden_dev],
        share2[:, hidden_dev:].T,
        grad_time,
        sums[n_seqs] * factor,
        sums[n_seqs + 1] * factor,
    )


def solution(mesh):
    in_specs = (
        P("dp", None, None),
        P("dp", None),
        P("dp", None),
        P("dp"),
        P(None, "dp", "tensor"),
        P("tensor", "dp"),
        P("dp", "tensor"),
        P("tensor", "dp"),
        P(None, "dp"),
        P("dp"),
        P("dp"),
        P("dp", None, None),
    )
    out_specs = (
        P("dp", None, "tensor"),
        P("dp", None, "tensor"),
        P(None, "dp", "tensor"),
        P("tensor", "dp"),
        P("dp", "tensor"),
        P("tensor", "dp"),
        P(None, "dp"),
        P("dp"),
        P("dp"),
    )
    return jax.shard_map(shards, mesh=mesh, in_specs=in_specs, out_specs=out_specs, check_vma=False)
```

profile of v0, /device:TPU:0, one launch (start us, length us, event | category | flops | bytes accessed | tf_op | source)
XLA Modules:
  0.0 683.9 jit_solution(16655282718602888327)
XLA Ops:
  14.9 12.1 %all-reduce = s32[16]{0:T(128)S(1)} all-reduce(s32[16]{0:T(128)S(1)} %dynamic-update-slice), channel_id=1, replica_groups=mesh['dp'=8,'tensor'=4] {'dp'}, use_global_device_ids=true, to_apply=%add | all-reduce | flops 16 | bytes 128
  28.4 31.2 %all_gather.10 = f32[18,1024]{1,0:T(8,128)S(1)} all-gather(f32[18,128]{1,0:T(8,128)S(1)} %pad_maximum_fusion.10), channel_id=1, replica_groups=mesh['dp'=8,'tensor'=4] {'dp'}, dimensions={1}, use_global_device_ids=true | all-gather | bytes 82944 | tf_op jit(solution)/shard_map/all_gather | solution.py:191
  64.4 16.2 %multiply_sine_fusion.1 = (f32[1024,512]{1,0:T(8,128)S(1)}, f32[1024,512]{1,0:T(8,128)S(1)}, f32[1024,512]{1,0:T(8,128)}, f32[1024,512]{1,0:T(8,128)}) fusion(f32[512]{0:T(512)S(1)} %multiply_exponential_fusion, f32[1024]{0:T(1024)S(1)} %get-tuple-element.168, f32[1024]{0:T(1024)S(1)} %get-tuple-element.166), kind=kLoop, calls=%fused_computation.119 | loop fusion | flops 1048576 | bytes 8398848 | tf_op jit(solution)/shard_map/sin | solution.py:19
  118.0 7.5 %fusion.238 = (f32[4,1024]{1,0:T(4,128)S(1)}, f32[4,1024,1024]{1,2,0:T(8,128)}) fusion(bf16[1024,4,64]{0,2,1:T(8,128)(2,1)S(1)} %bitcast.178, bf16[1024,4,64]{0,2,1:T(8,128)(2,1)S(1)} %bitcast.176, pred[1024,1024]{0,1:T(8,128)(4,1)S(1)} %broadcast_compare_fusion.1), kind=kOutput, calls=%fused_computation.439 | convolution fusion | flops 549449728 | bytes 18890752 | tf_op jit(solution)/shard_map/qhe,khe->hqk/dot_general | solution.py:48
  125.5 8.0 %fusion = f32[4,1024]{1,0:T(4,128)S(1)} fusion(f32[4,1024,1024]{1,2,0:T(8,128)} %get-tuple-element.152, f32[4,1024]{1,0:T(4,128)S(1)} %get-tuple-element.151), kind=kLoop, calls=%fused_computation.12 | loop fusion | flops 8384512 | bytes 16809984 | tf_op jit(solution)/shard_map/reduce_sum | solution.py:52
  133.5 7.6 %fusion.144 = bf16[4,64,1024]{2,1,0:T(8,128)(2,1)S(1)} fusion(bf16[1024,4,64]{0,2,1:T(8,128)(2,1)S(1)} %bitcast.188, f32[4,1024,1024]{1,2,0:T(8,128)} %get-tuple-element.152, f32[4,1024]{1,0:T(4,128)S(1)} %fusion, f32[4,1024]{1,0:T(4,128)S(1)} %get-tuple-element.151), kind=kOutput, calls=%fused_computation.250 | convolution fusion | flops 549715968 | bytes 17858560 | tf_op jit(solution)/shard_map/hqk,khe->qhe/dot_general | solution.py:54
  146.3 23.7 %collective-permute-done.8 = bf16[512,1024]{1,0:T(8,128)(2,1)S(1)} collective-permute-done((bf16[512,1024]{1,0:T(8,128)(2,1)S(1)}, bf16[512,1024]{1,0:T(8,128)(2,1)S(1)}, u32[]{:S(2)}, u32[]{:S(2)}) %collective-permute-start.8) | collective-permute-done | bytes 1048608 | tf_op jit(solution)/shard_map/ppermute | solution.py:133
  206.0 12.1 %collective-permute-done.18 = bf16[512,1024]{1,0:T(8,128)(2,1)} collective-permute-done((bf16[512,1024]{1,0:T(8,128)(2,1)S(1)}, bf16[512,1024]{1,0:T(8,128)(2,1)}, u32[]{:S(2)}, u32[]{:S(2)}) %collective-permute-start.18) | collective-permute-done | bytes 1048608 | tf_op jit(solution)/shard_map/ppermute | solution.py:133
  229.7 9.4 %fusion.124 = bf16[4,64,1024]{2,1,0:T(8,128)(2,1)} fusion(bf16[1024,4,64]{0,2,1:T(8,128)(2,1)S(1)} %bitcast.182, f32[4,1024,1024]{1,2,0:T(8,128)} %get-tuple-element.152, f32[4,1024]{1,0:T(4,128)S(1)} %log_add_fusion.1), kind=kOutput, calls=%fused_computation.240 | convolution fusion | flops 545521664 | bytes 17842176 | tf_op jit(solution)/shard_map/hqk,qhe->khe/dot_general | solution.py:63
  239.1 7.6 %multiply_reduce_fusion.1 = (f32[4,1024]{1,0:T(4,128)S(1)}, f32[4,1024,1024]{1,2,0:T(8,128)}) fusion(f32[4,1024,1024]{1,2,0:T(8,128)S(1)} %bitcast.171, f32[4,1024]{1,0:T(4,128)S(1)} %log_add_fusion.1, bf16[1024,4,64]{0,2,1:T(8,128)(2,1)S(1)} %bitcast.183, bf16[1024,4,64]{0,2,1:T(8,128)(2,1)S(1)} %bitcast.189), kind=kOutput, calls=%fused_computation.4 | convolution fusion | flops 549449728 | bytes 34635776 | tf_op jit(solution)/shard_map/qhe,khe->hqk/dot_general | solution.py:62
  246.7 8.3 %multiply_convert_fusion.1 = bf16[4,1024,1024]{1,2,0:T(8,128)(2,1)S(1)} fusion(f32[4,1024,1024]{1,2,0:T(8,128)} %get-tuple-element.156, f32[4,1024,1024]{1,2,0:T(8,128)S(1)} %bitcast.171, f32[4,1024]{1,0:T(4,128)S(1)} %get-tuple-element.155, f32[4,1024]{1,0:T(4,128)S(1)} %log_add_fusion.1), kind=kLoop, calls=%fused_computation.3 | loop fusion | flops 16777216 | bytes 41975808 | tf_op jit(solution)/shard_map/convert_element_type | solution.py:65
  270.1 7.5 %fusion.239 = (f32[4,1024]{1,0:T(4,128)S(1)}, f32[4,1024,1024]{1,2,0:T(8,128)}) fusion(bf16[1024,4,64]{0,2,1:T(8,128)(2,1)S(1)} %bitcast.174, bf16[1024,4,64]{0,2,1:T(8,128)(2,1)S(1)} %bitcast.172, pred[1024,1024]{0,1:T(8,128)(4,1)S(1)} %broadcast_compare_fusion), kind=kOutput, calls=%fused_computation.440 | convolution fusion | flops 549449728 | bytes 18890752 | tf_op jit(solution)/shard_map/qhe,khe->hqk/dot_general | solution.py:48
  277.5 8.0 %fusion.1 = f32[4,1024]{1,0:T(4,128)S(1)} fusion(f32[4,1024,1024]{1,2,0:T(8,128)} %get-tuple-element.159, f32[4,1024]{1,0:T(4,128)S(1)} %get-tuple-element.158), kind=kLoop, calls=%fused_computation.13 | loop fusion | flops 8384512 | bytes 16809984 | tf_op jit(solution)/shard_map/reduce_sum | solution.py:52
  285.6 7.7 %fusion.143 = bf16[4,64,1024]{2,1,0:T(8,128)(2,1)S(1)} fusion(bf16[1024,4,64]{0,2,1:T(8,128)(2,1)S(1)} %bitcast.186, f32[4,1024,1024]{1,2,0:T(8,128)} %get-tuple-element.159, f32[4,1024]{1,0:T(4,128)S(1)} %fusion.1, f32[4,1024]{1,0:T(4,128)S(1)} %get-tuple-element.158), kind=kOutput, calls=%fused_computation.249 | convolution fusion | flops 549715968 | bytes 17858560 | tf_op jit(solution)/shard_map/hqk,khe->qhe/dot_general | solution.py:54
  298.5 23.7 %collective-permute-done.13 = bf16[512,1024]{1,0:T(8,128)(2,1)S(1)} collective-permute-done((bf16[512,1024]{1,0:T(8,128)(2,1)S(1)}, bf16[512,1024]{1,0:T(8,128)(2,1)S(1)}, u32[]{:S(2)}, u32[]{:S(2)}) %collective-permute-start.13) | collective-permute-done | bytes 1048608 | tf_op jit(solution)/shard_map/ppermute | solution.py:133
  380.8 9.4 %fusion.89 = bf16[1024,1024]{0,1:T(8,128)(2,1)} fusion(bf16[1024,1024]{1,0:T(8,128)(2,1)} %get-tuple-element.160, bf16[1024,1024]{1,0:T(8,128)(2,1)} %copy-done.109, bf16[1024,1024]{1,0:T(8,128)(2,1)} %fusion.67, bf16[1024,1024]{1,0:T(8,128)(2,1)} %fusion.68), kind=kOutput, calls=%fused_computation.203 | convolution fusion | flops 4312793088 | bytes 10485760 | tf_op jit(solution)/shard_map/ki,kj->ij/dot_general | solution.py:80
  403.2 9.2 %fusion.94 = bf16[1024,1024]{0,1:T(8,128)(2,1)} fusion(bf16[1024,1024]{1,0:T(8,128)(2,1)} %copy-done.108, bf16[1024,1024]{1,0:T(8,128)(2,1)} %copy-done.107, bf16[512,1024]{1,0:T(8,128)(2,1)} %collective-permute-done.14, bf16[512,1024]{1,0:T(8,128)(2,1)} %multiply_convert_fusion.6, bf16[512,1024]{1,0:T(8,128)(2,1)} %collective-permute-done.9, ...), kind=kOutput, calls=%fused_computation.204 | convolution fusion | flops 4321181696 | bytes 10485760 | tf_op jit(solution)/shard_map/ki,kj->ij/dot_general | solution.py:80
  419.0 10.5 %multiply_reduce_fusion = (f32[4,1024]{1,0:T(4,128)S(1)}, f32[4,1024,1024]{1,2,0:T(8,128)}) fusion(f32[4,1024,1024]{1,2,0:T(8,128)S(1)} %bitcast.169, f32[4,1024]{1,0:T(4,128)S(1)} %log_add_fusion, bf16[1024,4,64]{0,2,1:T(8,128)(2,1)} %bitcast.185, bf16[1024,4,64]{0,2,1:T(8,128)(2,1)} %bitcast.187), kind=kOutput, calls=%fused_computation.1 | convolution fusion | flops 549449728 | bytes 34635776 | tf_op jit(solution)/shard_map/qhe,khe->hqk/dot_general | solution.py:62
  429.6 8.0 %multiply_convert_fusion = bf16[4,1024,1024]{1,2,0:T(8,128)(2,1)S(1)} fusion(f32[4,1024,1024]{1,2,0:T(8,128)} %get-tuple-element.163, f32[4,1024,1024]{1,2,0:T(8,128)S(1)} %bitcast.169, f32[4,1024]{1,0:T(4,128)S(1)} %get-tuple-element.162, f32[4,1024]{1,0:T(4,128)S(1)} %log_add_fusion), kind=kLoop, calls=%fused_computation | loop fusion | flops 16777216 | bytes 41975808 | tf_op jit(solution)/shard_map/convert_element_type | solution.py:65
  483.2 7.7 %collective-permute-done.21 = bf16[1024,1,256]{2,0,1:T(8,128)(2,1)} collective-permute-done((bf16[1024,1,256]{2,0,1:T(8,128)(2,1)}, bf16[1024,1,256]{2,0,1:T(8,128)(2,1)}, u32[]{:S(2)}, u32[]{:S(2)}) %collective-permute-start.21) | collective-permute-done | bytes 524320 | tf_op jit(solution)/shard_map/ppermute | solution.py:133
  520.4 49.7 %all-reduce.3.cloned.1.call-done = f32[18,1024]{1,0:T(8,128)} async-done(((f32[18,1024]{1,0:T(8,128)}), f32[18,1024]{1,0:T(8,128)}) %all-reduce.3.cloned.1.call-update) | async-done | bytes 73744 | tf_op jit(solution)/shard_map/psum | solution.py:312
  585.8 14.7 %collective-permute-done.32 = bf16[128,1024]{0,1:T(8,128)(2,1)S(1)} collective-permute-done((bf16[128,1024]{0,1:T(8,128)(2,1)S(1)}, bf16[128,1024]{0,1:T(8,128)(2,1)S(1)}, u32[]{:S(2)}, u32[]{:S(2)}) %collective-permute-start.32) | collective-permute-done | bytes 262176 | tf_op jit(solution)/shard_map/ppermute | solution.py:124
  604.5 16.3 %collective-permute-done.33 = bf16[128,1024]{0,1:T(8,128)(2,1)S(1)} collective-permute-done((bf16[128,1024]{0,1:T(8,128)(2,1)S(1)}, bf16[128,1024]{0,1:T(8,128)(2,1)S(1)}, u32[]{:S(2)}, u32[]{:S(2)}) %collective-permute-start.33) | collective-permute-done | bytes 262176 | tf_op jit(solution)/shard_map/ppermute | solution.py:124
  625.9 47.9 %reduce-scatter.4.cloned.1.call-done = bf16[128,2048]{1,0:T(8,128)(2,1)} async-done(((bf16[1024,2048]{1,0:T(8,128)(2,1)}), bf16[128,2048]{1,0:T(8,128)(2,1)}) %reduce-scatter.4.cloned.1.call-update) | async-done | bytes 524304
  (495 shorter events, 290.1 us)
Async XLA Ops:
  7.2 171.6 %all-gather.2.cloned.1.call-start = ((), (), s32[]{:S(2)}) async-start(), calls=%async_computation.1 | async-start | bytes 4718592 | tf_op jit(solution)/shard_map/all_gather | solution.py:184
  9.1 77.5 %collective-permute-start = (bf16[128,1024]{0,1:T(8,128)(2,1)S(1)}, bf16[128,1024]{0,1:T(8,128)(2,1)}, u32[]{:S(2)}, u32[]{:S(2)}) collective-permute-start(bf16[128,1024]{0,1:T(8,128)(2,1)S(1)} %get-tuple-element.117), channel_id=1, source_target_pairs={{8,0},{16,8},{24,16},{28,24},{20,28},{12,20},{4,12},{0,4},{9,1},{1... | collective-permute-start | bytes 786440 | tf_op jit(solution)/shard_map/ppermute | solution.py:106
  12.1 74.6 %collective-permute-start.1 = (bf16[128,1024]{0,1:T(8,128)(2,1)S(1)}, bf16[128,1024]{0,1:T(8,128)(2,1)S(1)}, u32[]{:S(2)}, u32[]{:S(2)}) collective-permute-start(bf16[128,1024]{0,1:T(8,128)(2,1)S(1)} %get-tuple-element.117), channel_id=1, source_target_pairs={{0,8},{8,16},{16,24},{24,28},{28,20},{20,12},{12,4},{4,0},{1,9},{9... | collective-permute-start | bytes 786440 | tf_op jit(solution)/shard_map/ppermute | solution.py:104
  13.3 556.8 %all-reduce.3.cloned.1.call-start = ((), (), s32[]{:S(2)}) async-start(), calls=%async_computation.2 | async-start | bytes 196608 | tf_op jit(solution)/shard_map/psum | solution.py:312
  86.6 17.2 %collective-permute-start.2 = (bf16[128,1024]{0,1:T(8,128)(2,1)}, bf16[128,1024]{0,1:T(8,128)(2,1)}, u32[]{:S(2)}, u32[]{:S(2)}) collective-permute-start(bf16[128,1024]{0,1:T(8,128)(2,1)} %collective-permute-done), channel_id=1, source_target_pairs={{8,0},{16,8},{24,16},{28,24},{20,28},{12,20},{4,12},{0,4},{9,1},{1... | collective-permute-start | bytes 786440 | tf_op jit(solution)/shard_map/ppermute | solution.py:106
  86.6 15.7 %collective-permute-start.3 = (bf16[128,1024]{0,1:T(8,128)(2,1)S(1)}, bf16[128,1024]{0,1:T(8,128)(2,1)}, u32[]{:S(2)}, u32[]{:S(2)}) collective-permute-start(bf16[128,1024]{0,1:T(8,128)(2,1)S(1)} %collective-permute-done.1), channel_id=1, source_target_pairs={{0,8},{8,16},{16,24},{24,28},{28,20},{20,12},{12,4},{4,0},{1,9},{9... | collective-permute-start | bytes 786440 | tf_op jit(solution)/shard_map/ppermute | solution.py:104
  144.7 25.3 %collective-permute-start.8 = (bf16[512,1024]{1,0:T(8,128)(2,1)S(1)}, bf16[512,1024]{1,0:T(8,128)(2,1)S(1)}, u32[]{:S(2)}, u32[]{:S(2)}) collective-permute-start(bf16[512,1024]{1,0:T(8,128)(2,1)S(1)} %add_convert_fusion.5), channel_id=1, source_target_pairs={{0,2},{1,3},{2,0},{3,1},{4,6},{5,7},{6,4},{7,5},{8,10},{9,11},{10,... | collective-permute-start | bytes 3145736 | tf_op jit(solution)/shard_map/ppermute | solution.py:133
  192.7 25.4 %collective-permute-start.18 = (bf16[512,1024]{1,0:T(8,128)(2,1)S(1)}, bf16[512,1024]{1,0:T(8,128)(2,1)}, u32[]{:S(2)}, u32[]{:S(2)}) collective-permute-start(bf16[512,1024]{1,0:T(8,128)(2,1)S(1)} %add_convert_fusion.1), channel_id=1, source_target_pairs={{0,2},{1,3},{2,0},{3,1},{4,6},{5,7},{6,4},{7,5},{8,10},{9,11},{10,... | collective-permute-start | bytes 3145736 | tf_op jit(solution)/shard_map/ppermute | solution.py:133
  296.9 25.3 %collective-permute-start.13 = (bf16[512,1024]{1,0:T(8,128)(2,1)S(1)}, bf16[512,1024]{1,0:T(8,128)(2,1)S(1)}, u32[]{:S(2)}, u32[]{:S(2)}) collective-permute-start(bf16[512,1024]{1,0:T(8,128)(2,1)S(1)} %add_convert_fusion.3), channel_id=1, source_target_pairs={{0,2},{1,3},{2,0},{3,1},{4,6},{5,7},{6,4},{7,5},{8,10},{9,11},{10,... | collective-permute-start | bytes 3145736 | tf_op jit(solution)/shard_map/ppermute | solution.py:133
  324.3 15.6 %collective-permute-start.14 = (bf16[512,1024]{1,0:T(8,128)(2,1)}, bf16[512,1024]{1,0:T(8,128)(2,1)}, u32[]{:S(2)}, u32[]{:S(2)}) collective-permute-start(bf16[512,1024]{1,0:T(8,128)(2,1)} %multiply_convert_fusion.6), channel_id=1, source_target_pairs={{0,1},{1,0},{2,3},{3,2},{4,5},{5,4},{6,7},{7,6},{8,9},{9,8},{10,11... | collective-permute-start | bytes 3145736 | tf_op jit(solution)/shard_map/ppermute | solution.py:133
  339.5 121.9 %collective-permute-start.10 = (bf16[1024,2,256]{2,0,1:T(8,128)(2,1)}, bf16[1024,2,256]{2,0,1:T(8,128)(2,1)}, u32[]{:S(2)}, u32[]{:S(2)}) collective-permute-start(bf16[1024,2,256]{2,0,1:T(8,128)(2,1)} %fusion.154), channel_id=1, source_target_pairs={{0,1},{1,0},{2,3},{3,2},{4,5},{5,4},{6,7},{7,6},{8,9},{9,8},{10,11... | collective-permute-start | bytes 3145736 | tf_op jit(solution)/shard_map/ppermute | solution.py:133
  365.6 100.3 %collective-permute-start.20 = (bf16[1024,2,256]{2,0,1:T(8,128)(2,1)}, bf16[1024,2,256]{2,0,1:T(8,128)(2,1)}, u32[]{:S(2)}, u32[]{:S(2)}) collective-permute-start(bf16[1024,2,256]{2,0,1:T(8,128)(2,1)} %dynamic-slice_bitcast_fusion.1), channel_id=1, source_target_pairs={{0,1},{1,0},{2,3},{3,2},{4,5},{5,4},{6,7},{7,6},{8,9},{9,8},{10,11... | collective-permute-start | bytes 3145736 | tf_op jit(solution)/shard_map/ppermute | solution.py:133
  370.4 25.7 %collective-permute-start.23 = (bf16[512,1024]{1,0:T(8,128)(2,1)}, bf16[512,1024]{1,0:T(8,128)(2,1)}, u32[]{:S(2)}, u32[]{:S(2)}) collective-permute-start(bf16[512,1024]{1,0:T(8,128)(2,1)} %add_convert_fusion), channel_id=1, source_target_pairs={{0,2},{1,3},{2,0},{3,1},{4,6},{5,7},{6,4},{7,5},{8,10},{9,11},{10,... | collective-permute-start | bytes 3145736 | tf_op jit(solution)/shard_map/ppermute | solution.py:133
  450.2 223.6 %reduce-scatter.4.cloned.1.call-start = ((), (), s32[]{:S(2)}) async-start(), calls=%async_computation.3 | async-start | bytes 4718592
  464.4 15.1 %collective-permute-start.11 = (bf16[1024,1,256]{2,0,1:T(8,128)(2,1)}, bf16[1024,1,256]{2,0,1:T(8,128)(2,1)}, u32[]{:S(2)}, u32[]{:S(2)}) collective-permute-start(bf16[1024,1,256]{2,0,1:T(8,128)(2,1)} %dynamic-slice_convert_fusion.3), channel_id=1, source_target_pairs={{0,2},{1,3},{2,0},{3,1},{4,6},{5,7},{6,4},{7,5},{8,10},{9,11},{10,... | collective-permute-start | bytes 1572872 | tf_op jit(solution)/shard_map/ppermute | solution.py:133
  473.2 23.1 %collective-permute-start.15 = (bf16[1024,2,256]{2,0,1:T(8,128)(2,1)}, bf16[1024,2,256]{2,0,1:T(8,128)(2,1)S(1)}, u32[]{:S(2)}, u32[]{:S(2)}) collective-permute-start(bf16[1024,2,256]{2,0,1:T(8,128)(2,1)} %fusion.150), channel_id=1, source_target_pairs={{0,1},{1,0},{2,3},{3,2},{4,5},{5,4},{6,7},{7,6},{8,9},{9,8},{10,11... | collective-permute-start | bytes 3145736 | tf_op jit(solution)/shard_map/ppermute | solution.py:133
  497.7 80.0 %collective-permute-start.16 = (bf16[1024,1,256]{2,0,1:T(8,128)(2,1)}, bf16[1024,1,256]{2,0,1:T(8,128)(2,1)}, u32[]{:S(2)}, u32[]{:S(2)}) collective-permute-start(bf16[1024,1,256]{2,0,1:T(8,128)(2,1)} %dynamic-slice_convert_fusion.2), channel_id=1, source_target_pairs={{0,2},{1,3},{2,0},{3,1},{4,6},{5,7},{6,4},{7,5},{8,10},{9,11},{10,... | collective-permute-start | bytes 1572872 | tf_op jit(solution)/shard_map/ppermute | solution.py:133
  507.7 71.2 %collective-permute-start.31 = (bf16[128,1024]{0,1:T(8,128)(2,1)}, bf16[128,1024]{0,1:T(8,128)(2,1)S(1)}, u32[]{:S(2)}, u32[]{:S(2)}) collective-permute-start(bf16[128,1024]{0,1:T(8,128)(2,1)} %get-tuple-element.90), channel_id=1, source_target_pairs={{8,0},{16,8},{24,16},{28,24},{20,28},{12,20},{4,12},{0,4},{9,1},{1... | collective-permute-start | bytes 786440 | tf_op jit(solution)/shard_map/ppermute | solution.py:124
  517.4 54.6 %collective-permute-start.28 = (bf16[128,1024]{0,1:T(8,128)(2,1)}, bf16[128,1024]{0,1:T(8,128)(2,1)}, u32[]{:S(2)}, u32[]{:S(2)}) collective-permute-start(bf16[128,1024]{0,1:T(8,128)(2,1)} %add_convert_fusion.12), channel_id=1, source_target_pairs={{0,8},{8,16},{16,24},{24,28},{28,20},{20,12},{12,4},{4,0},{1,9},{9... | collective-permute-start | bytes 786440 | tf_op jit(solution)/shard_map/ppermute | solution.py:124
  520.4 80.2 %collective-permute-start.25 = (bf16[1024,2,256]{2,0,1:T(8,128)(2,1)}, bf16[1024,2,256]{2,0,1:T(8,128)(2,1)S(1)}, u32[]{:S(2)}, u32[]{:S(2)}) collective-permute-start(bf16[1024,2,256]{2,0,1:T(8,128)(2,1)} %dynamic-slice_bitcast_fusion), channel_id=1, source_target_pairs={{0,1},{1,0},{2,3},{3,2},{4,5},{5,4},{6,7},{7,6},{8,9},{9,8},{10,11... | collective-permute-start | bytes 3145736 | tf_op jit(solution)/shard_map/ppermute | solution.py:133
  581.0 19.4 %collective-permute-start.32 = (bf16[128,1024]{0,1:T(8,128)(2,1)S(1)}, bf16[128,1024]{0,1:T(8,128)(2,1)S(1)}, u32[]{:S(2)}, u32[]{:S(2)}) collective-permute-start(bf16[128,1024]{0,1:T(8,128)(2,1)S(1)} %get-tuple-element.88), channel_id=1, source_target_pairs={{8,0},{16,8},{24,16},{28,24},{20,28},{12,20},{4,12},{0,4},{9,1},{1... | collective-permute-start | bytes 786440 | tf_op jit(solution)/shard_map/ppermute | solution.py:124
  585.2 19.2 %collective-permute-start.30 = (bf16[128,1024]{0,1:T(8,128)(2,1)S(1)}, bf16[128,1024]{0,1:T(8,128)(2,1)S(1)}, u32[]{:S(2)}, u32[]{:S(2)}) collective-permute-start(bf16[128,1024]{0,1:T(8,128)(2,1)S(1)} %get-tuple-element.87), channel_id=1, source_target_pairs={{0,8},{8,16},{16,24},{24,28},{28,20},{20,12},{12,4},{4,0},{1,9},{9... | collective-permute-start | bytes 786440 | tf_op jit(solution)/shard_map/ppermute | solution.py:124
  600.5 20.2 %collective-permute-start.33 = (bf16[128,1024]{0,1:T(8,128)(2,1)S(1)}, bf16[128,1024]{0,1:T(8,128)(2,1)S(1)}, u32[]{:S(2)}, u32[]{:S(2)}) collective-permute-start(bf16[128,1024]{0,1:T(8,128)(2,1)S(1)} %add_convert_fusion.8), channel_id=1, source_target_pairs={{8,0},{16,8},{24,16},{28,24},{20,28},{12,20},{4,12},{0,4},{9,1},{1... | collective-permute-start | bytes 786440 | tf_op jit(solution)/shard_map/ppermute | solution.py:124
  602.5 20.1 %collective-permute-start.26 = (bf16[1024,1,256]{2,0,1:T(8,128)(2,1)S(1)}, bf16[1024,1,256]{2,0,1:T(8,128)(2,1)S(1)}, u32[]{:S(2)}, u32[]{:S(2)}) collective-permute-start(bf16[1024,1,256]{2,0,1:T(8,128)(2,1)S(1)} %dynamic-slice_convert_fusion), channel_id=1, source_target_pairs={{0,2},{1,3},{2,0},{3,1},{4,6},{5,7},{6,4},{7,5},{8,10},{9,11},{10,... | collective-permute-start | bytes 1572872 | tf_op jit(solution)/shard_map/ppermute | solution.py:133
  (132 other events, 960.9 us)
Sparse Core Ops, SparseCore 0:
  13.4 80.6 all-gather.1
  450.4 119.6 all-reduce.2
  573.7 100.0 reduce-scatter.3
where the time goes:
time: 692 us; the launch traced here: 684 us
  waiting for transfers between devices  223 us (32%)
  matrix products  145 us (21%)
  other arithmetic  122 us (18%)
  local copies, waits for them, and re-layouts  90.8 us (13%)
  blocking collectives  43.3 us (6%)
  starting transfers between devices  30.4 us (4%)
  between operations  29.9 us (4%)
    ppermute x20, waiting for transfers between devices, swap(): return lax.ppermute(value, 'tensor', [(i, i ^ bit) for i in range(n)])  82.7 us
    psum x1, waiting for transfers between devices, shards(): sums = lax.psum(sums, ('dp', 'tensor'))  49.7 us
    unnamed x4, waiting for transfers between devices  47.9 us
    unnamed x253, local copies, waits for them, and re-layouts  38.4 us
    ppermute x7, waiting for transfers between devices, scatter(): run = lax.ppermute(run.astype(bf16), 'dp', way).astype(f32)  35.6 us
    all_gather x1, blocking collectives, shards(): small = lax.all_gather(small, 'dp', axis=1, tiled=True)  31.2 us
    dot_general x8, matrix products, mm(): return jnp.dot(left, right, preferred_element_type=f32)  26.2 us
    dot_general x4, matrix products, mm_lt(): return jnp.einsum('ki,kj->ij', left, right, preferred_element_type=f32)  25 us
  transfers between devices with their start and end apart: 37, of which 18 were waited for; matrix products, arithmetic and copies ran while one was open for 36% of the time, Pallas kernels for 0%

commit v1 on v0

--- a/solution.py
+++ b/solution.py
@@ -309,7 +309,7 @@
     sums = jnp.zeros((n_seqs, width), f32)
     sums = lax.dynamic_update_slice_in_dim(sums, jnp.stack(seq_sums), me_dp * seqs_dev, 0)
     sums = jnp.concatenate([sums, gain_attn_sum[None], gain_mlp_sum[None] * (1.0 / chips)], axis=0)
-    sums = lax.psum(sums, ("dp", "tensor"))
+    sums = lax.psum(lax.psum(sums, "tensor"), "dp")
     rows = width // n_dp
     sums = lax.dynamic_slice_in_dim(sums, me_dp * rows, rows, 1)
     factor = float(n_seqs * seq_len) ** (-0.5)

time: 692 us -> 665 us (0.961)
  waiting for transfers between devices: 223 us -> 202 us
    psum x1 -> x2, waiting for transfers between devices: 49.7 us -> 24.7 us  [shards(): sums = lax.psum(lax.psum(sums, 'tensor'), 'dp')]
    unnamed x4 -> x5, waiting for transfers between devices: 47.9 us -> 51.2 us
    unnamed x253 -> x259, local copies, waits for them, and re-layouts: 38.4 us -> 38.4 us
  transfers between devices with their start and end apart: 37 -> 38, of which waited for: 18 -> 18; matrix products, arithmetic and copies ran while one was open for 36% -> 36% of each run, Pallas kernels for 0% -> 0%
where the time goes in v1:
time: 665 us; the launch traced here: 657 us
  waiting for transfers between devices  202 us (30%)
  matrix products  141 us (21%)
  other arithmetic  121 us (18%)
  local copies, waits for them, and re-layouts  92.3 us (14%)
  blocking collectives  43.3 us (7%)
  between operations  30.3 us (5%)
  starting transfers between devices  27.1 us (4%)
    ppermute x20, waiting for transfers between devices, swap(): return lax.ppermute(value, 'tensor', [(i, i ^ bit) for i in range(n)])  88.2 us
    unnamed x5, waiting for transfers between devices  51.2 us
    unnamed x259, local copies, waits for them, and re-layouts  38.4 us
    all_gather x1, blocking collectives, shards(): small = lax.all_gather(small, 'dp', axis=1, tiled=True)  31.2 us
    ppermute x7, waiting for transfers between devices, scatter(): run = lax.ppermute(run.astype(bf16), 'dp', way).astype(f32)  30.7 us
    psum x2, waiting for transfers between devices, shards(): sums = lax.psum(lax.psum(sums, 'tensor'), 'dp')  24.7 us
    dot_general x8, matrix products, mm(): return jnp.dot(left, right, preferred_element_type=f32)  24.2 us
    dot_general x4, matrix products, mm_lt(): return jnp.einsum('ki,kj->ij', left, right, preferred_element_type=f32)  23.8 us
  transfers between devices with their start and end apart: 38, of which 18 were waited for; matrix products, arithmetic and copies ran while one was open for 36% of the time, Pallas kernels for 0%

profile of v1, /device:TPU:0, one launch (start us, length us, event | category | flops | bytes accessed | tf_op | source)
XLA Modules:
  0.0 657.2 jit_solution(4835459991298632572)
XLA Ops:
  14.9 12.1 %all-reduce = s32[16]{0:T(128)S(1)} all-reduce(s32[16]{0:T(128)S(1)} %dynamic-update-slice), channel_id=1, replica_groups=mesh['dp'=8,'tensor'=4] {'dp'}, use_global_device_ids=true, to_apply=%add | all-reduce | flops 16 | bytes 128
  28.4 31.2 %all_gather.10 = f32[18,1024]{1,0:T(8,128)S(1)} all-gather(f32[18,128]{1,0:T(8,128)S(1)} %pad_maximum_fusion.10), channel_id=1, replica_groups=mesh['dp'=8,'tensor'=4] {'dp'}, dimensions={1}, use_global_device_ids=true | all-gather | bytes 82944 | tf_op jit(solution)/shard_map/all_gather | solution.py:191
  64.4 16.2 %multiply_sine_fusion.1 = (f32[1024,512]{1,0:T(8,128)S(1)}, f32[1024,512]{1,0:T(8,128)S(1)}, f32[1024,512]{1,0:T(8,128)}, f32[1024,512]{1,0:T(8,128)}) fusion(f32[512]{0:T(512)S(1)} %multiply_exponential_fusion, f32[1024]{0:T(1024)S(1)} %get-tuple-element.168, f32[1024]{0:T(1024)S(1)} %get-tuple-element.166), kind=kLoop, calls=%fused_computation.119 | loop fusion | flops 1048576 | bytes 8398848 | tf_op jit(solution)/shard_map/sin | solution.py:19
  118.1 7.4 %fusion.238 = (f32[4,1024]{1,0:T(4,128)S(1)}, f32[4,1024,1024]{1,2,0:T(8,128)}) fusion(bf16[1024,4,64]{0,2,1:T(8,128)(2,1)S(1)} %bitcast.178, bf16[1024,4,64]{0,2,1:T(8,128)(2,1)S(1)} %bitcast.176, pred[1024,1024]{0,1:T(8,128)(4,1)S(1)} %broadcast_compare_fusion.1), kind=kOutput, calls=%fused_computation.439 | convolution fusion | flops 549449728 | bytes 18890752 | tf_op jit(solution)/shard_map/qhe,khe->hqk/dot_general | solution.py:48
  125.5 8.0 %fusion = f32[4,1024]{1,0:T(4,128)S(1)} fusion(f32[4,1024,1024]{1,2,0:T(8,128)} %get-tuple-element.152, f32[4,1024]{1,0:T(4,128)S(1)} %get-tuple-element.151), kind=kLoop, calls=%fused_computation.12 | loop fusion | flops 8384512 | bytes 16809984 | tf_op jit(solution)/shard_map/reduce_sum | solution.py:52
  133.5 7.6 %fusion.144 = bf16[4,64,1024]{2,1,0:T(8,128)(2,1)S(1)} fusion(bf16[1024,4,64]{0,2,1:T(8,128)(2,1)S(1)} %bitcast.188, f32[4,1024,1024]{1,2,0:T(8,128)} %get-tuple-element.152, f32[4,1024]{1,0:T(4,128)S(1)} %fusion, f32[4,1024]{1,0:T(4,128)S(1)} %get-tuple-element.151), kind=kOutput, calls=%fused_computation.250 | convolution fusion | flops 549715968 | bytes 17858560 | tf_op jit(solution)/shard_map/hqk,khe->qhe/dot_general | solution.py:54
  146.3 23.7 %collective-permute-done.8 = bf16[512,1024]{1,0:T(8,128)(2,1)S(1)} collective-permute-done((bf16[512,1024]{1,0:T(8,128)(2,1)S(1)}, bf16[512,1024]{1,0:T(8,128)(2,1)S(1)}, u32[]{:S(2)}, u32[]{:S(2)}) %collective-permute-start.8) | collective-permute-done | bytes 1048608 | tf_op jit(solution)/shard_map/ppermute | solution.py:133
  206.1 12.0 %collective-permute-done.18 = bf16[512,1024]{1,0:T(8,128)(2,1)} collective-permute-done((bf16[512,1024]{1,0:T(8,128)(2,1)S(1)}, bf16[512,1024]{1,0:T(8,128)(2,1)}, u32[]{:S(2)}, u32[]{:S(2)}) %collective-permute-start.18) | collective-permute-done | bytes 1048608 | tf_op jit(solution)/shard_map/ppermute | solution.py:133
  229.2 9.4 %fusion.124 = bf16[4,64,1024]{2,1,0:T(8,128)(2,1)} fusion(bf16[1024,4,64]{0,2,1:T(8,128)(2,1)S(1)} %bitcast.182, f32[4,1024,1024]{1,2,0:T(8,128)} %get-tuple-element.152, f32[4,1024]{1,0:T(4,128)S(1)} %log_add_fusion.1), kind=kOutput, calls=%fused_computation.240 | convolution fusion | flops 545521664 | bytes 17842176 | tf_op jit(solution)/shard_map/hqk,qhe->khe/dot_general | solution.py:63
  238.6 7.6 %multiply_reduce_fusion.1 = (f32[4,1024]{1,0:T(4,128)S(1)}, f32[4,1024,1024]{1,2,0:T(8,128)}) fusion(f32[4,1024,1024]{1,2,0:T(8,128)S(1)} %bitcast.171, f32[4,1024]{1,0:T(4,128)S(1)} %log_add_fusion.1, bf16[1024,4,64]{0,2,1:T(8,128)(2,1)S(1)} %bitcast.183, bf16[1024,4,64]{0,2,1:T(8,128)(2,1)S(1)} %bitcast.189), kind=kOutput, calls=%fused_computation.4 | convolution fusion | flops 549449728 | bytes 34635776 | tf_op jit(solution)/shard_map/qhe,khe->hqk/dot_general | solution.py:62
  246.2 8.3 %multiply_convert_fusion.1 = bf16[4,1024,1024]{1,2,0:T(8,128)(2,1)S(1)} fusion(f32[4,1024,1024]{1,2,0:T(8,128)} %get-tuple-element.156, f32[4,1024,1024]{1,2,0:T(8,128)S(1)} %bitcast.171, f32[4,1024]{1,0:T(4,128)S(1)} %get-tuple-element.155, f32[4,1024]{1,0:T(4,128)S(1)} %log_add_fusion.1), kind=kLoop, calls=%fused_computation.3 | loop fusion | flops 16777216 | bytes 41975808 | tf_op jit(solution)/shard_map/convert_element_type | solution.py:65
  276.5 8.0 %fusion.1 = f32[4,1024]{1,0:T(4,128)S(1)} fusion(f32[4,1024,1024]{1,2,0:T(8,128)} %get-tuple-element.159, f32[4,1024]{1,0:T(4,128)S(1)} %get-tuple-element.158), kind=kLoop, calls=%fused_computation.13 | loop fusion | flops 8384512 | bytes 16809984 | tf_op jit(solution)/shard_map/reduce_sum | solution.py:52
  284.6 7.7 %fusion.143 = bf16[4,64,1024]{2,1,0:T(8,128)(2,1)S(1)} fusion(bf16[1024,4,64]{0,2,1:T(8,128)(2,1)S(1)} %bitcast.186, f32[4,1024,1024]{1,2,0:T(8,128)} %get-tuple-element.159, f32[4,1024]{1,0:T(4,128)S(1)} %fusion.1, f32[4,1024]{1,0:T(4,128)S(1)} %get-tuple-element.158), kind=kOutput, calls=%fused_computation.249 | convolution fusion | flops 549715968 | bytes 17858560 | tf_op jit(solution)/shard_map/hqk,khe->qhe/dot_general | solution.py:54
  297.5 23.7 %collective-permute-done.13 = bf16[512,1024]{1,0:T(8,128)(2,1)S(1)} collective-permute-done((bf16[512,1024]{1,0:T(8,128)(2,1)S(1)}, bf16[512,1024]{1,0:T(8,128)(2,1)S(1)}, u32[]{:S(2)}, u32[]{:S(2)}) %collective-permute-start.13) | collective-permute-done | bytes 1048608 | tf_op jit(solution)/shard_map/ppermute | solution.py:133
  379.4 12.4 %collective-permute-done.23 = bf16[512,1024]{1,0:T(8,128)(2,1)} collective-permute-done((bf16[512,1024]{1,0:T(8,128)(2,1)}, bf16[512,1024]{1,0:T(8,128)(2,1)}, u32[]{:S(2)}, u32[]{:S(2)}) %collective-permute-start.23) | collective-permute-done | bytes 1048608 | tf_op jit(solution)/shard_map/ppermute | solution.py:133
  398.5 8.6 %fusion.89 = bf16[1024,1024]{0,1:T(8,128)(2,1)} fusion(bf16[1024,1024]{1,0:T(8,128)(2,1)} %get-tuple-element.160, bf16[1024,1024]{1,0:T(8,128)(2,1)} %copy-done.112, bf16[1024,1024]{1,0:T(8,128)(2,1)S(1)} %copy-done.42, bf16[1024,1024]{1,0:T(8,128)(2,1)S(1)} %copy-done.40), kind=kOutput, calls=%fused_computation.203 | convolution fusion | flops 4312793088 | bytes 10485760 | tf_op jit(solution)/shard_map/ki,kj->ij/dot_general | solution.py:80
  413.5 10.5 %multiply_reduce_fusion = (f32[4,1024]{1,0:T(4,128)S(1)}, f32[4,1024,1024]{1,2,0:T(8,128)}) fusion(f32[4,1024,1024]{1,2,0:T(8,128)S(1)} %bitcast.169, f32[4,1024]{1,0:T(4,128)S(1)} %log_add_fusion, bf16[1024,4,64]{0,2,1:T(8,128)(2,1)} %bitcast.185, bf16[1024,4,64]{0,2,1:T(8,128)(2,1)} %bitcast.187), kind=kOutput, calls=%fused_computation.1 | convolution fusion | flops 549449728 | bytes 34635776 | tf_op jit(solution)/shard_map/qhe,khe->hqk/dot_general | solution.py:62
  424.0 8.0 %multiply_convert_fusion = bf16[4,1024,1024]{1,2,0:T(8,128)(2,1)S(1)} fusion(f32[4,1024,1024]{1,2,0:T(8,128)} %get-tuple-element.163, f32[4,1024,1024]{1,2,0:T(8,128)S(1)} %bitcast.169, f32[4,1024]{1,0:T(4,128)S(1)} %get-tuple-element.162, f32[4,1024]{1,0:T(4,128)S(1)} %log_add_fusion), kind=kLoop, calls=%fused_computation | loop fusion | flops 16777216 | bytes 41975808 | tf_op jit(solution)/shard_map/convert_element_type | solution.py:65
  444.6 9.2 %fusion.94 = bf16[1024,1024]{0,1:T(8,128)(2,1)} fusion(bf16[1024,1024]{1,0:T(8,128)(2,1)} %copy-done.110, bf16[1024,1024]{1,0:T(8,128)(2,1)} %copy-done.109, bf16[512,1024]{1,0:T(8,128)(2,1)} %copy-done.105, bf16[512,1024]{1,0:T(8,128)(2,1)} %copy-done.71, bf16[512,1024]{1,0:T(8,128)(2,1)} %collective-permute-done.9, bf16[512,1024]{1,0:T(8,128)(2,1)S(1)} %copy-done.68), kind=kOutput, calls=%fused_computation.204 | convolution fusion | flops 4321181696 | bytes 10485760 | tf_op jit(solution)/shard_map/ki,kj->ij/dot_general | solution.py:80
  453.7 20.9 %all-reduce.4.cloned.1.call-done = f32[18,1024]{1,0:T(8,128)} async-done(((f32[18,1024]{1,0:T(8,128)}), f32[18,1024]{1,0:T(8,128)}) %all-reduce.4.cloned.1.call-update) | async-done | bytes 73744 | tf_op jit(solution)/shard_map/psum | solution.py:312
  505.2 8.0 %collective-permute-done.21 = bf16[1024,1,256]{2,0,1:T(8,128)(2,1)} collective-permute-done((bf16[1024,1,256]{2,0,1:T(8,128)(2,1)}, bf16[1024,1,256]{2,0,1:T(8,128)(2,1)}, u32[]{:S(2)}, u32[]{:S(2)}) %collective-permute-start.21) | collective-permute-done | bytes 524320 | tf_op jit(solution)/shard_map/ppermute | solution.py:133
  562.2 14.6 %collective-permute-done.32 = bf16[128,1024]{0,1:T(8,128)(2,1)S(1)} collective-permute-done((bf16[128,1024]{0,1:T(8,128)(2,1)S(1)}, bf16[128,1024]{0,1:T(8,128)(2,1)S(1)}, u32[]{:S(2)}, u32[]{:S(2)}) %collective-permute-start.32) | collective-permute-done | bytes 262176 | tf_op jit(solution)/shard_map/ppermute | solution.py:124
  580.3 10.3 %collective-permute-done.33 = bf16[128,1024]{0,1:T(8,128)(2,1)S(1)} collective-permute-done((bf16[128,1024]{0,1:T(8,128)(2,1)S(1)}, bf16[128,1024]{0,1:T(8,128)(2,1)S(1)}, u32[]{:S(2)}, u32[]{:S(2)}) %collective-permute-start.33) | collective-permute-done | bytes 262176 | tf_op jit(solution)/shard_map/ppermute | solution.py:124
  595.8 51.2 %reduce-scatter.4.cloned.1.call-done = bf16[128,2048]{1,0:T(8,128)(2,1)} async-done(((bf16[1024,2048]{1,0:T(8,128)(2,1)}), bf16[128,2048]{1,0:T(8,128)(2,1)}) %reduce-scatter.4.cloned.1.call-update) | async-done | bytes 524304
  (504 shorter events, 290.2 us)
Async XLA Ops:
  7.2 171.8 %all-gather.2.cloned.1.call-start = ((), (), s32[]{:S(2)}) async-start(), calls=%async_computation.1 | async-start | bytes 4718592 | tf_op jit(solution)/shard_map/all_gather | solution.py:184
  9.1 77.5 %collective-permute-start = (bf16[128,1024]{0,1:T(8,128)(2,1)S(1)}, bf16[128,1024]{0,1:T(8,128)(2,1)}, u32[]{:S(2)}, u32[]{:S(2)}) collective-permute-start(bf16[128,1024]{0,1:T(8,128)(2,1)S(1)} %get-tuple-element.117), channel_id=1, source_target_pairs={{8,0},{16,8},{24,16},{28,24},{20,28},{12,20},{4,12},{0,4},{9,1},{1... | collective-permute-start | bytes 786440 | tf_op jit(solution)/shard_map/ppermute | solution.py:106
  12.1 74.5 %collective-permute-start.1 = (bf16[128,1024]{0,1:T(8,128)(2,1)S(1)}, bf16[128,1024]{0,1:T(8,128)(2,1)S(1)}, u32[]{:S(2)}, u32[]{:S(2)}) collective-permute-start(bf16[128,1024]{0,1:T(8,128)(2,1)S(1)} %get-tuple-element.117), channel_id=1, source_target_pairs={{0,8},{8,16},{16,24},{24,28},{28,20},{20,12},{12,4},{4,0},{1,9},{9... | collective-permute-start | bytes 786440 | tf_op jit(solution)/shard_map/ppermute | solution.py:104
  13.3 461.4 %all-reduce.4.cloned.1.call-start = ((), (), s32[]{:S(2)}) async-start(), calls=%async_computation.2 | async-start | bytes 196608 | tf_op jit(solution)/shard_map/psum | solution.py:312
  86.6 17.3 %collective-permute-start.2 = (bf16[128,1024]{0,1:T(8,128)(2,1)}, bf16[128,1024]{0,1:T(8,128)(2,1)}, u32[]{:S(2)}, u32[]{:S(2)}) collective-permute-start(bf16[128,1024]{0,1:T(8,128)(2,1)} %collective-permute-done), channel_id=1, source_target_pairs={{8,0},{16,8},{24,16},{28,24},{20,28},{12,20},{4,12},{0,4},{9,1},{1... | collective-permute-start | bytes 786440 | tf_op jit(solution)/shard_map/ppermute | solution.py:106
  86.6 15.8 %collective-permute-start.3 = (bf16[128,1024]{0,1:T(8,128)(2,1)S(1)}, bf16[128,1024]{0,1:T(8,128)(2,1)}, u32[]{:S(2)}, u32[]{:S(2)}) collective-permute-start(bf16[128,1024]{0,1:T(8,128)(2,1)S(1)} %collective-permute-done.1), channel_id=1, source_target_pairs={{0,8},{8,16},{16,24},{24,28},{28,20},{20,12},{12,4},{4,0},{1,9},{9... | collective-permute-start | bytes 786440 | tf_op jit(solution)/shard_map/ppermute | solution.py:104
  144.8 25.3 %collective-permute-start.8 = (bf16[512,1024]{1,0:T(8,128)(2,1)S(1)}, bf16[512,1024]{1,0:T(8,128)(2,1)S(1)}, u32[]{:S(2)}, u32[]{:S(2)}) collective-permute-start(bf16[512,1024]{1,0:T(8,128)(2,1)S(1)} %add_convert_fusion.5), channel_id=1, source_target_pairs={{0,2},{1,3},{2,0},{3,1},{4,6},{5,7},{6,4},{7,5},{8,10},{9,11},{10,... | collective-permute-start | bytes 3145736 | tf_op jit(solution)/shard_map/ppermute | solution.py:133
  192.8 25.4 %collective-permute-start.18 = (bf16[512,1024]{1,0:T(8,128)(2,1)S(1)}, bf16[512,1024]{1,0:T(8,128)(2,1)}, u32[]{:S(2)}, u32[]{:S(2)}) collective-permute-start(bf16[512,1024]{1,0:T(8,128)(2,1)S(1)} %add_convert_fusion.1), channel_id=1, source_target_pairs={{0,2},{1,3},{2,0},{3,1},{4,6},{5,7},{6,4},{7,5},{8,10},{9,11},{10,... | collective-permute-start | bytes 3145736 | tf_op jit(solution)/shard_map/ppermute | solution.py:133
  295.9 25.3 %collective-permute-start.13 = (bf16[512,1024]{1,0:T(8,128)(2,1)S(1)}, bf16[512,1024]{1,0:T(8,128)(2,1)S(1)}, u32[]{:S(2)}, u32[]{:S(2)}) collective-permute-start(bf16[512,1024]{1,0:T(8,128)(2,1)S(1)} %add_convert_fusion.3), channel_id=1, source_target_pairs={{0,2},{1,3},{2,0},{3,1},{4,6},{5,7},{6,4},{7,5},{8,10},{9,11},{10,... | collective-permute-start | bytes 3145736 | tf_op jit(solution)/shard_map/ppermute | solution.py:133
  336.7 25.1 %collective-permute-start.22 = (bf16[512,1024]{1,0:T(8,128)(2,1)}, bf16[512,1024]{1,0:T(8,128)(2,1)}, u32[]{:S(2)}, u32[]{:S(2)}) collective-permute-start(bf16[512,1024]{1,0:T(8,128)(2,1)} %convolution_convert_fusion.2), channel_id=1, source_target_pairs={{0,1},{1,0},{2,3},{3,2},{4,5},{5,4},{6,7},{7,6},{8,9},{9,8},{10,11... | collective-permute-start | bytes 3145736 | tf_op jit(solution)/shard_map/ppermute | solution.py:133
  347.3 138.3 %collective-permute-start.10 = (bf16[1024,2,256]{2,0,1:T(8,128)(2,1)}, bf16[1024,2,256]{2,0,1:T(8,128)(2,1)}, u32[]{:S(2)}, u32[]{:S(2)}) collective-permute-start(bf16[1024,2,256]{2,0,1:T(8,128)(2,1)} %fusion.154), channel_id=1, source_target_pairs={{0,1},{1,0},{2,3},{3,2},{4,5},{5,4},{6,7},{7,6},{8,9},{9,8},{10,11... | collective-permute-start | bytes 3145736 | tf_op jit(solution)/shard_map/ppermute | solution.py:133
  366.4 25.4 %collective-permute-start.23 = (bf16[512,1024]{1,0:T(8,128)(2,1)}, bf16[512,1024]{1,0:T(8,128)(2,1)}, u32[]{:S(2)}, u32[]{:S(2)}) collective-permute-start(bf16[512,1024]{1,0:T(8,128)(2,1)} %add_convert_fusion), channel_id=1, source_target_pairs={{0,2},{1,3},{2,0},{3,1},{4,6},{5,7},{6,4},{7,5},{8,10},{9,11},{10,... | collective-permute-start | bytes 3145736 | tf_op jit(solution)/shard_map/ppermute | solution.py:133
  370.5 118.3 %collective-permute-start.20 = (bf16[1024,2,256]{2,0,1:T(8,128)(2,1)}, bf16[1024,2,256]{2,0,1:T(8,128)(2,1)}, u32[]{:S(2)}, u32[]{:S(2)}) collective-permute-start(bf16[1024,2,256]{2,0,1:T(8,128)(2,1)} %dynamic-slice_bitcast_fusion.1), channel_id=1, source_target_pairs={{0,1},{1,0},{2,3},{3,2},{4,5},{5,4},{6,7},{7,6},{8,9},{9,8},{10,11... | collective-permute-start | bytes 3145736 | tf_op jit(solution)/shard_map/ppermute | solution.py:133
  444.5 103.3 %all-reduce.6.cloned.1.call-start = ((), (), s32[]{:S(2)}) async-start(), calls=%async_computation.3 | async-start | bytes 196608 | tf_op jit(solution)/shard_map/psum | solution.py:312
  474.7 172.3 %reduce-scatter.4.cloned.1.call-start = ((), (), s32[]{:S(2)}) async-start(), calls=%async_computation.4 | async-start | bytes 4718592
  496.5 22.1 %collective-permute-start.15 = (bf16[1024,2,256]{2,0,1:T(8,128)(2,1)}, bf16[1024,2,256]{2,0,1:T(8,128)(2,1)S(1)}, u32[]{:S(2)}, u32[]{:S(2)}) collective-permute-start(bf16[1024,2,256]{2,0,1:T(8,128)(2,1)} %fusion.150), channel_id=1, source_target_pairs={{0,1},{1,0},{2,3},{3,2},{4,5},{5,4},{6,7},{7,6},{8,9},{9,8},{10,11... | collective-permute-start | bytes 3145736 | tf_op jit(solution)/shard_map/ppermute | solution.py:133
  498.6 14.7 %collective-permute-start.21 = (bf16[1024,1,256]{2,0,1:T(8,128)(2,1)}, bf16[1024,1,256]{2,0,1:T(8,128)(2,1)}, u32[]{:S(2)}, u32[]{:S(2)}) collective-permute-start(bf16[1024,1,256]{2,0,1:T(8,128)(2,1)} %dynamic-slice_convert_fusion.1), channel_id=1, source_target_pairs={{0,2},{1,3},{2,0},{3,1},{4,6},{5,7},{6,4},{7,5},{8,10},{9,11},{10,... | collective-permute-start | bytes 1572872 | tf_op jit(solution)/shard_map/ppermute | solution.py:133
  519.9 33.4 %collective-permute-start.16 = (bf16[1024,1,256]{2,0,1:T(8,128)(2,1)}, bf16[1024,1,256]{2,0,1:T(8,128)(2,1)}, u32[]{:S(2)}, u32[]{:S(2)}) collective-permute-start(bf16[1024,1,256]{2,0,1:T(8,128)(2,1)} %dynamic-slice_convert_fusion.2), channel_id=1, source_target_pairs={{0,2},{1,3},{2,0},{3,1},{4,6},{5,7},{6,4},{7,5},{8,10},{9,11},{10,... | collective-permute-start | bytes 1572872 | tf_op jit(solution)/shard_map/ppermute | solution.py:133
  531.2 23.3 %collective-permute-start.31 = (bf16[128,1024]{0,1:T(8,128)(2,1)}, bf16[128,1024]{0,1:T(8,128)(2,1)S(1)}, u32[]{:S(2)}, u32[]{:S(2)}) collective-permute-start(bf16[128,1024]{0,1:T(8,128)(2,1)} %get-tuple-element.90), channel_id=1, source_target_pairs={{8,0},{16,8},{24,16},{28,24},{20,28},{12,20},{4,12},{0,4},{9,1},{1... | collective-permute-start | bytes 786440 | tf_op jit(solution)/shard_map/ppermute | solution.py:124
  544.1 32.8 %collective-permute-start.25 = (bf16[1024,2,256]{2,0,1:T(8,128)(2,1)}, bf16[1024,2,256]{2,0,1:T(8,128)(2,1)S(1)}, u32[]{:S(2)}, u32[]{:S(2)}) collective-permute-start(bf16[1024,2,256]{2,0,1:T(8,128)(2,1)} %dynamic-slice_bitcast_fusion), channel_id=1, source_target_pairs={{0,1},{1,0},{2,3},{3,2},{4,5},{5,4},{6,7},{7,6},{8,9},{9,8},{10,11... | collective-permute-start | bytes 3145736 | tf_op jit(solution)/shard_map/ppermute | solution.py:133
  557.6 19.1 %collective-permute-start.32 = (bf16[128,1024]{0,1:T(8,128)(2,1)S(1)}, bf16[128,1024]{0,1:T(8,128)(2,1)S(1)}, u32[]{:S(2)}, u32[]{:S(2)}) collective-permute-start(bf16[128,1024]{0,1:T(8,128)(2,1)S(1)} %get-tuple-element.88), channel_id=1, source_target_pairs={{8,0},{16,8},{24,16},{28,24},{20,28},{12,20},{4,12},{0,4},{9,1},{1... | collective-permute-start | bytes 786440 | tf_op jit(solution)/shard_map/ppermute | solution.py:124
  561.0 19.3 %collective-permute-start.30 = (bf16[128,1024]{0,1:T(8,128)(2,1)S(1)}, bf16[128,1024]{0,1:T(8,128)(2,1)S(1)}, u32[]{:S(2)}, u32[]{:S(2)}) collective-permute-start(bf16[128,1024]{0,1:T(8,128)(2,1)S(1)} %get-tuple-element.87), channel_id=1, source_target_pairs={{0,8},{8,16},{16,24},{24,28},{28,20},{20,12},{12,4},{4,0},{1,9},{9... | collective-permute-start | bytes 786440 | tf_op jit(solution)/shard_map/ppermute | solution.py:124
  576.9 13.8 %collective-permute-start.33 = (bf16[128,1024]{0,1:T(8,128)(2,1)S(1)}, bf16[128,1024]{0,1:T(8,128)(2,1)S(1)}, u32[]{:S(2)}, u32[]{:S(2)}) collective-permute-start(bf16[128,1024]{0,1:T(8,128)(2,1)S(1)} %add_convert_fusion.8), channel_id=1, source_target_pairs={{8,0},{16,8},{24,16},{28,24},{20,28},{12,20},{4,12},{0,4},{9,1},{1... | collective-permute-start | bytes 786440 | tf_op jit(solution)/shard_map/ppermute | solution.py:124
  578.8 13.6 %collective-permute-start.26 = (bf16[1024,1,256]{2,0,1:T(8,128)(2,1)S(1)}, bf16[1024,1,256]{2,0,1:T(8,128)(2,1)S(1)}, u32[]{:S(2)}, u32[]{:S(2)}) collective-permute-start(bf16[1024,1,256]{2,0,1:T(8,128)(2,1)S(1)} %dynamic-slice_convert_fusion), channel_id=1, source_target_pairs={{0,2},{1,3},{2,0},{3,1},{4,6},{5,7},{6,4},{7,5},{8,10},{9,11},{10,... | collective-permute-start | bytes 1572872 | tf_op jit(solution)/shard_map/ppermute | solution.py:133
  (136 other events, 901.3 us)
Sparse Core Ops, SparseCore 0:
  13.4 80.5 all-gather.1
  444.6 29.9 all-reduce.3
  478.4 69.3 all-reduce.5
  551.8 95.1 reduce-scatter.3
